TPU v7x, 32 devices: a whole 2x2x4 slice. The times are simulated.
32 devices in a mesh: dom: 8 (over y, x, core), sub: 4 (over z).
Axes of the slice: x: 2, y: 2, z: 4, core: 2. Of those that a mesh axis runs over, the one named last changes fastest.
Arguments:
- start_dofs: float32 [140, 8192], P(None, ('dom', 'sub')), may hold values from -6 to 6
- inv_jac: float32 [9, 8192], P(None, ('dom', 'sub')), may hold values from -2 to 2
- normals: float32 [12, 8192], P(None, ('dom', 'sub')), may hold values from -3.5 to 3.5
- bulk_modulus: float32 [8192], P(('dom', 'sub')), may hold values from 0.5 to 2
- density: float32 [8192], P(('dom', 'sub')), may hold values from 0.5 to 2
- deriv_mats: float32 [3, 35, 35], replicated, may hold values from -1 to 1
- face_proj: float32 [4, 15, 35], replicated, may hold values from -1 to 1
- face_lift: float32 [4, 35, 15], replicated, may hold values from -1 to 1
- cluster: int32 [8192], P(('dom', 'sub')), may hold values from 0 to 1, as said below
- pml_flags: int32 [8192], P(('dom', 'sub')), may hold values 0 or 1
- neighbours: int32 [4, 8192], P(None, ('dom', 'sub')), may hold values from 0 to 1343, as said below
- dom_send: int32 [64, 96], P(('dom', 'sub')), may hold values from 0 to 1023, as said below
- sub_send: int32 [128, 32], P(('dom', 'sub')), may hold values from 0 to 1022, as said below
Outputs:
- final_dofs: float32 [140, 8192], P(None, ('dom', 'sub'))
Inputs may be any that keep to these rules, and one draw needn't show every extreme that they name: `cluster`: on every device the fine elements come first among its 256 elements; a device holds at most 64 of them, and some device exactly 64. `neighbours`: each face names one column of its device's trace pool. Own faces that are not listed for sending name each other in pairs. The face at place j of dom_send row 0 names place j of the block from the device before, the one at place j of row 1 place j of the block from the device after; the face at place j of the sub_send row for device b names place j of the block from b, or place j + 1 - 2 (j % 2) when b is the device itself. `dom_send`: together with its sub_send rows, the rows of one device list distinct columns of its own faces; every device lists its last face column here. `sub_send`: together with its dom_send rows, the rows of one device list distinct columns of its own faces; every device lists its second-to-last face column here.
All inputs are finite; a program needn't handle non-finite values. No bound on the sum of `pml_flags` on one device may be relied on, other than what follows from the above.
Results may differ from a plain program's by a relative error of at most 0.0003.
Values sent between devices are 32-bit elements; how exact they have to be, the bound alone decides.
No kernel may reach another device: no remote copies, remote signals or barrier semaphores. Data moves between devices by JAX's collectives and lax.ppermute only.
A program may use at most 64 MiB of HBM per device.

v0:
```python
import math
import jax
import jax.numpy as jnp
from jax import lax
from jax.sharding import PartitionSpec as P

NQ = 4
NB = 35
ORDER = 5
SUBSTEPS = 4
exact_dots = lax.Precision.HIGHEST
step_size = 0.8
sigma_pml = 1.5


def from_behind(shard, axis, by):
    peers = lax.axis_size(axis)
    pairs = [(i, i + by) for i in range(peers) if 0 <= i + by < peers]
    return lax.ppermute(shard, axis, pairs)


def apply_operator(coeffs, material):
    inv_jac, bulk_modulus, density, damping, deriv_mats = material
    n_basis = deriv_mats.shape[1]
    pressure = coeffs[0]
    velocity = coeffs[1:]
    stacked = deriv_mats.reshape(3 * n_basis, n_basis)
    d_press = jnp.dot(stacked, pressure, precision=exact_dots).reshape(3, n_basis, -1)
    jacobian = inv_jac.reshape(3, 3, -1)
    gradient = jnp.sum(jacobian[:, :, None, :] * d_press[:, None, :, :], axis=0)
    mixed_vel = jnp.sum(jacobian[:, :, None, :] * velocity[None, :, :, :], axis=1)
    joined = jnp.transpose(deriv_mats, (1, 0, 2)).reshape(n_basis, 3 * n_basis)
    diverg = jnp.dot(joined, mixed_vel.reshape(3 * n_basis, -1), precision=exact_dots)
    press_rate = -bulk_modulus * diverg - damping * pressure
    veloc_rate = -gradient / density - damping * velocity
    return jnp.concatenate([press_rate[None], veloc_rate], axis=0)


def taylor(coeffs, material):
    deriv_terms = [coeffs]
    for power in range(ORDER - 1):
        deriv_terms.append(apply_operator(deriv_terms[-1], material))
    return deriv_terms


def integrate(deriv_terms, start_time, end_time):
    summed = None
    for power, taylor_term in enumerate(deriv_terms):
        weight = (end_time ** (power + 1) - start_time ** (power + 1)) / math.factorial(power + 1)
        scaled = weight * taylor_term
        summed = scaled if summed is None else summed + scaled
    return summed


def face_traces(coeffs, face_proj):
    face_parts = []
    for face_idx in range(4):
        traced = jnp.einsum("kb,qbe->kqe", face_proj[face_idx], coeffs, precision=exact_dots)
        face_parts.append(traced.reshape(-1, coeffs.shape[2]))
    return jnp.concatenate(face_parts, axis=1)


def corrections(own_traces, nbr_traces, normals, bulk_modulus, density, face_lift):
    n_elem = normals.shape[1]
    n_face = face_lift.shape[2]
    jump_all = (nbr_traces - own_traces).reshape(n_face, 4, 4, n_elem)
    jump_press = jump_all[:, 0]
    jump_vel = jump_all[:, 1:]
    facing = jnp.transpose(normals.reshape(4, 3, n_elem), (1, 0, 2))
    normal_flow = jnp.sum(facing[None] * jump_vel, axis=1)
    sound_speed = jnp.sqrt(bulk_modulus / density)
    penalty = sound_speed * jnp.sqrt(jnp.sum(facing * facing, axis=0))
    flux_press = 0.5 * (bulk_modulus * normal_flow - penalty * jump_press)
    flux_veloc = 0.5 * (facing[None] * jump_press[:, None] / density - penalty * jump_vel)
    flux_all = jnp.concatenate([flux_press[:, None], flux_veloc], axis=1)
    return jnp.einsum("fbk,kqfe->qbe", face_lift, flux_all, precision=exact_dots)


def gather_faces(own_traces, dom_send, sub_send):
    n_chan = own_traces.shape[0]
    n_sub = sub_send.shape[0]
    sub_width = sub_send.shape[1]
    dom_out = jnp.stack(
        [jnp.take(own_traces, dom_send[0], axis=1), jnp.take(own_traces, dom_send[1], axis=1)]
    )
    sub_out = jnp.take(own_traces, sub_send.reshape(-1), axis=1).reshape(n_chan, n_sub, sub_width)
    sub_in = lax.all_to_all(sub_out, "sub", split_axis=1, concat_axis=1, tiled=True).reshape(
        n_chan, n_sub * sub_width
    )
    from_below = from_behind(dom_out[1], "dom", 1)
    from_above = from_behind(dom_out[0], "dom", -1)
    return jnp.concatenate([own_traces, from_below, from_above, sub_in], axis=1)


def body(
    start_dofs,
    inv_jac,
    normals,
    bulk_modulus,
    density,
    deriv_mats,
    face_proj,
    face_lift,
    cluster,
    pml_flags,
    neighbours,
    dom_send,
    sub_send,
):
    n_elem = start_dofs.shape[1]
    dofs_zero = start_dofs.reshape(NQ, NB, n_elem)
    damping = sigma_pml * pml_flags.astype(jnp.float32)
    fine_mask = cluster == 1
    material = (inv_jac, bulk_modulus, density, damping, deriv_mats)
    coarse_terms = taylor(dofs_zero, material)
    sub_dt = step_size / SUBSTEPS
    head_material = (inv_jac, bulk_modulus, density, damping, deriv_mats)
    work_state = jnp.where(fine_mask, dofs_zero, 0.0)
    for sub_step in range(SUBSTEPS):
        coarse_part = integrate(coarse_terms, sub_step * sub_dt, (sub_step + 1) * sub_dt)
        work_head = work_state
        fine_part = integrate(taylor(work_head, head_material), 0.0, sub_dt)
        published = jnp.where(fine_mask, fine_part, coarse_part)
        own_traces = face_traces(published, face_proj)
        trace_pool = gather_faces(own_traces, dom_send, sub_send)
        nbr_traces = jnp.take(trace_pool, neighbours.reshape(-1), axis=1)
        lifted = corrections(own_traces, nbr_traces, normals, bulk_modulus, density, face_lift)
        coarse_next = work_state + lifted
        stepped = work_head + apply_operator(fine_part, head_material) - lifted
        head_next = jnp.where(fine_mask, stepped, coarse_next)
        work_state = head_next
    full_step = integrate(coarse_terms, 0.0, step_size)
    coarse_out = dofs_zero + apply_operator(full_step, material) - work_state
    return jnp.where(fine_mask, work_state, coarse_out).reshape(NQ * NB, n_elem)


def solution(mesh):
    in_specs = (
        P(None, ("dom", "sub")),
        P(None, ("dom", "sub")),
        P(None, ("dom", "sub")),
        P(("dom", "sub")),
        P(("dom", "sub")),
        P(),
        P(),
        P(),
        P(("dom", "sub")),
        P(("dom", "sub")),
        P(None, ("dom", "sub")),
        P(("dom", "sub"), None),
        P(("dom", "sub"), None),
    )
    out_specs = P(None, ("dom", "sub"))
    return jax.shard_map(body, mesh=mesh, in_specs=in_specs, out_specs=out_specs, check_vma=False)
```

profile of v0, /device:TPU:11, one launch (start us, length us, event | category | flops | bytes accessed | tf_op | source)
XLA Modules:
  0.0 125.4 jit_solution(3070285738189939827)
XLA Ops:
  0.0 0.8 reshape.421
  0.8 0.9 reshape.662
  1.7 0.9 slice.126
  2.9 0.6 copy-done.33
  3.7 0.6 copy-done.4
  4.3 0.6 divide_sqrt_fusion
  5.0 0.6 copy-done.2
  7.1 0.8 slice-done
  9.3 0.7 copy-done.13
  10.8 0.8 multiply_reduce_fusion.1
  15.3 0.6 gather_fusion.2
  16.0 0.7 reshape.663
  16.8 4.9 %all-to-all-start = ((f32[4,1,1920]{2,1,0:T(1,128)}), f32[4,1,1920]{2,1,0:T(1,128)S(1)}, u32[]{:S(2)}, u32[]{:S(2)}) async-start(f32[4,1,1920]{2,1,0:T(1,128)} %reshape.663), calls=%async_computation | async-start | bytes 61440 | tf_op jit(solution)/shard_map/all_to_all | solution.py:87
  21.7 0.7 copy-done.29
  22.4 0.6 gather_fusion
  23.1 4.2 %collective-permute-start = (f32[60,96]{0,1:T(8,128)S(1)}, f32[60,96]{0,1:T(8,128)S(1)}, u32[]{:S(2)}, u32[]{:S(2)}) collective-permute-start(f32[60,96]{0,1:T(8,128)S(1)} %select_bitcast_fusion.7), channel_id=1, source_target_pairs={{0,4},{4,8},{8,12},{12,16},{16,20},{20,24},{24,28},{1,5},{5,9},{9,... | collective-permute-start | bytes 69128 | tf_op jit(solution)/shard_map/ppermute | solution.py:19
  27.3 0.6 gather_fusion.1
  28.0 0.7 select_bitcast_fusion.6
  28.7 1.9 %collective-permute-start.1 = (f32[60,96]{0,1:T(8,128)}, f32[60,96]{0,1:T(8,128)}, u32[]{:S(2)}, u32[]{:S(2)}) collective-permute-start(f32[60,96]{0,1:T(8,128)} %select_bitcast_fusion.6), channel_id=1, source_target_pairs={{4,0},{8,4},{12,8},{16,12},{20,16},{24,20},{28,24},{5,1},{9,5},{13... | collective-permute-start | bytes 69128 | tf_op jit(solution)/shard_map/ppermute | solution.py:19
  30.9 0.7 copy-done.19
  32.5 0.6 copy-done.30
  33.2 2.1 %collective-permute-done.1 = f32[60,96]{0,1:T(8,128)} collective-permute-done((f32[60,96]{0,1:T(8,128)}, f32[60,96]{0,1:T(8,128)}, u32[]{:S(2)}, u32[]{:S(2)}) %collective-permute-start.1) | collective-permute-done | bytes 23072 | tf_op jit(solution)/shard_map/ppermute | solution.py:19
  35.3 0.8 constant_dynamic-update-slice_fusion.1
  36.1 0.5 broadcast.471
  36.6 0.6 reduce
  37.4 2.8 %gather_fusion.3 = f32[1024,60]{1,0:T(8,128)S(1)} fusion(f32[60,1344]{0,1:T(8,128)S(1)} %constant_dynamic-update-slice_fusion, s32[1024]{0:T(1024)S(1)} %get-tuple-element.102), kind=kCustom, calls=%fused_computation.2.clone | custom fusion | bytes 495616 | tf_op jit(solution)/shard_map/jit(_take)/gather | solution.py:126
  41.0 0.7 copy-done.5
  46.6 0.7 gather_fusion.5
  47.4 0.7 gather_fusion.4
  48.1 0.8 gather_fusion.6
  49.4 0.6 copy-done.28
  50.1 0.7 reshape.665
  50.9 4.5 %all-to-all-start.1 = ((f32[4,1,1920]{2,1,0:T(1,128)}), f32[4,1,1920]{2,1,0:T(1,128)S(1)}, u32[]{:S(2)}, u32[]{:S(2)}) async-start(f32[4,1,1920]{2,1,0:T(1,128)} %reshape.665), calls=%async_computation.1 | async-start | bytes 61440 | tf_op jit(solution)/shard_map/all_to_all | solution.py:87
  55.4 3.0 %collective-permute-start.2 = (f32[60,96]{0,1:T(8,128)S(1)}, f32[60,96]{0,1:T(8,128)S(1)}, u32[]{:S(2)}, u32[]{:S(2)}) collective-permute-start(f32[60,96]{0,1:T(8,128)S(1)} %select_bitcast_fusion.5), channel_id=1, source_target_pairs={{0,4},{4,8},{8,12},{12,16},{16,20},{20,24},{24,28},{1,5},{5,9},{9,... | collective-permute-start | bytes 69128 | tf_op jit(solution)/shard_map/ppermute | solution.py:19
  58.4 1.9 %collective-permute-start.3 = (f32[60,96]{0,1:T(8,128)S(1)}, f32[60,96]{0,1:T(8,128)S(1)}, u32[]{:S(2)}, u32[]{:S(2)}) collective-permute-start(f32[60,96]{0,1:T(8,128)S(1)} %select_bitcast_fusion.4), channel_id=1, source_target_pairs={{4,0},{8,4},{12,8},{16,12},{20,16},{24,20},{28,24},{5,1},{9,5},{13... | collective-permute-start | bytes 69128 | tf_op jit(solution)/shard_map/ppermute | solution.py:19
  60.4 4.3 %collective-permute-done.3 = f32[60,96]{0,1:T(8,128)S(1)} collective-permute-done((f32[60,96]{0,1:T(8,128)S(1)}, f32[60,96]{0,1:T(8,128)S(1)}, u32[]{:S(2)}, u32[]{:S(2)}) %collective-permute-start.3) | collective-permute-done | bytes 23072 | tf_op jit(solution)/shard_map/ppermute | solution.py:19
  64.7 0.6 reduce.1
  65.5 2.8 %gather_fusion.7 = f32[1024,60]{1,0:T(8,128)S(1)} fusion(f32[60,1344]{0,1:T(8,128)S(1)} %constant_dynamic-update-slice_fusion.7, s32[1024]{0:T(1024)S(1)} %get-tuple-element.102), kind=kCustom, calls=%fused_computation.13.clone | custom fusion | bytes 495616 | tf_op jit(solution)/shard_map/jit(_take)/gather | solution.py:126
  74.1 0.7 gather_fusion.9
  74.8 0.7 gather_fusion.8
  75.6 0.8 gather_fusion.10
  76.7 0.5 copy-done.23
  77.4 0.7 reshape.667
  78.3 4.5 %all-to-all-start.2 = ((f32[4,1,1920]{2,1,0:T(1,128)}), f32[4,1,1920]{2,1,0:T(1,128)S(1)}, u32[]{:S(2)}, u32[]{:S(2)}) async-start(f32[4,1,1920]{2,1,0:T(1,128)} %reshape.667), calls=%async_computation.2 | async-start | bytes 61440 | tf_op jit(solution)/shard_map/all_to_all | solution.py:87
  82.8 2.4 %collective-permute-start.4 = (f32[60,96]{0,1:T(8,128)S(1)}, f32[60,96]{0,1:T(8,128)S(1)}, u32[]{:S(2)}, u32[]{:S(2)}) collective-permute-start(f32[60,96]{0,1:T(8,128)S(1)} %select_bitcast_fusion.3), channel_id=1, source_target_pairs={{0,4},{4,8},{8,12},{12,16},{16,20},{20,24},{24,28},{1,5},{5,9},{9,... | collective-permute-start | bytes 69128 | tf_op jit(solution)/shard_map/ppermute | solution.py:19
  85.3 1.9 %collective-permute-start.5 = (f32[60,96]{0,1:T(8,128)S(1)}, f32[60,96]{0,1:T(8,128)S(1)}, u32[]{:S(2)}, u32[]{:S(2)}) collective-permute-start(f32[60,96]{0,1:T(8,128)S(1)} %select_bitcast_fusion.2), channel_id=1, source_target_pairs={{4,0},{8,4},{12,8},{16,12},{20,16},{24,20},{28,24},{5,1},{9,5},{13... | collective-permute-start | bytes 69128 | tf_op jit(solution)/shard_map/ppermute | solution.py:19
  87.3 4.3 %collective-permute-done.5 = f32[60,96]{0,1:T(8,128)S(1)} collective-permute-done((f32[60,96]{0,1:T(8,128)S(1)}, f32[60,96]{0,1:T(8,128)S(1)}, u32[]{:S(2)}, u32[]{:S(2)}) %collective-permute-start.5) | collective-permute-done | bytes 23072 | tf_op jit(solution)/shard_map/ppermute | solution.py:19
  91.6 0.6 reduce.2
  92.4 2.8 %gather_fusion.11 = f32[1024,60]{1,0:T(8,128)S(1)} fusion(f32[60,1344]{0,1:T(8,128)S(1)} %constant_dynamic-update-slice_fusion.14, s32[1024]{0:T(1024)S(1)} %get-tuple-element.102), kind=kCustom, calls=%fused_computation.14.clone | custom fusion | bytes 495616 | tf_op jit(solution)/shard_map/jit(_take)/gather | solution.py:126
  95.9 0.7 copy-done.15
  99.6 0.5 copy-done.12
  100.4 0.5 copy-done.10
  101.1 0.5 copy-done.8
  103.0 0.7 gather_fusion.13
  103.8 0.7 gather_fusion.12
  104.5 0.8 gather_fusion.14
  106.0 0.7 reshape.669
  106.7 4.5 %all-to-all-start.3 = ((f32[4,1,1920]{2,1,0:T(1,128)}), f32[4,1,1920]{2,1,0:T(1,128)S(1)}, u32[]{:S(2)}, u32[]{:S(2)}) async-start(f32[4,1,1920]{2,1,0:T(1,128)} %reshape.669), calls=%async_computation.3 | async-start | bytes 61440 | tf_op jit(solution)/shard_map/all_to_all | solution.py:87
  111.2 2.4 %collective-permute-start.6 = (f32[60,96]{0,1:T(8,128)S(1)}, f32[60,96]{0,1:T(8,128)S(1)}, u32[]{:S(2)}, u32[]{:S(2)}) collective-permute-start(f32[60,96]{0,1:T(8,128)S(1)} %select_bitcast_fusion.1), channel_id=1, source_target_pairs={{0,4},{4,8},{8,12},{12,16},{16,20},{20,24},{24,28},{1,5},{5,9},{9,... | collective-permute-start | bytes 69128 | tf_op jit(solution)/shard_map/ppermute | solution.py:19
  113.7 1.9 %collective-permute-start.7 = (f32[60,96]{0,1:T(8,128)S(1)}, f32[60,96]{0,1:T(8,128)S(1)}, u32[]{:S(2)}, u32[]{:S(2)}) collective-permute-start(f32[60,96]{0,1:T(8,128)S(1)} %select_bitcast_fusion), channel_id=1, source_target_pairs={{4,0},{8,4},{12,8},{16,12},{20,16},{24,20},{28,24},{5,1},{9,5},{13... | collective-permute-start | bytes 69128 | tf_op jit(solution)/shard_map/ppermute | solution.py:19
  115.7 4.3 %collective-permute-done.7 = f32[60,96]{0,1:T(8,128)S(1)} collective-permute-done((f32[60,96]{0,1:T(8,128)S(1)}, f32[60,96]{0,1:T(8,128)S(1)}, u32[]{:S(2)}, u32[]{:S(2)}) %collective-permute-start.7) | collective-permute-done | bytes 23072 | tf_op jit(solution)/shard_map/ppermute | solution.py:19
  120.0 0.6 reduce.3
  120.8 2.8 %gather_fusion.15 = f32[1024,60]{1,0:T(8,128)S(1)} fusion(f32[60,1344]{0,1:T(8,128)S(1)} %constant_dynamic-update-slice_fusion.21, s32[1024]{0:T(1024)S(1)} %get-tuple-element.102), kind=kCustom, calls=%fused_computation.15.clone | custom fusion | bytes 495616 | tf_op jit(solution)/shard_map/jit(_take)/gather | solution.py:126
  124.7 0.7 reshape.447
  (368 shorter events, 28.5 us)
Async XLA Ops:
  0.8 15.2 %copy-start.27 = (pred[128]{0:T(512)(128)(4,1)}, pred[128]{0:T(512)(128)(4,1)S(1)}, u32[]{:S(2)}) copy-start(pred[128]{0:T(512)(128)(4,1)S(1)} %compare_and_fusion.1) | copy-start | bytes 388
  0.8 1.8 %copy-start.1 = (f32[140,256]{1,0:T(8,128)S(1)}, f32[140,256]{1,0:T(8,128)}, u32[]{:S(2)}) copy-start(f32[140,256]{1,0:T(8,128)} %param.19) | copy-start | bytes 430084
  1.7 0.9 copy-start
  2.9 0.7 copy-start.33
  2.9 0.7 copy-start.18
  3.6 0.7 copy-start.4
  3.6 0.7 copy-start.14
  3.7 0.7 copy-start.32
  5.0 0.7 copy-start.2
  7.0 0.9 slice-start
  9.3 0.8 copy-start.13
  9.3 0.9 copy-start.3
  10.0 5.2 %copy-start.25 = (s32[1024]{0:T(1024)}, s32[1024]{0:T(1024)S(1)}, u32[]{:S(2)}) copy-start(s32[1024]{0:T(1024)S(1)} %pad_clamp_fusion) | copy-start | bytes 12292
  10.1 62.1 %copy-start.11 = (f32[1,15,35]{2,0,1:T(1,128)}, f32[1,15,35]{2,0,1:T(1,128)S(1)}, u32[]{:S(2)}) copy-start(f32[1,15,35]{2,0,1:T(1,128)S(1)} %get-tuple-element.91) | copy-start | bytes 6304
  10.1 62.3 %copy-start.9 = (f32[1,15,35]{2,0,1:T(1,128)}, f32[1,15,35]{2,0,1:T(1,128)S(1)}, u32[]{:S(2)}) copy-start(f32[1,15,35]{2,0,1:T(1,128)S(1)} %get-tuple-element.92) | copy-start | bytes 6304
  10.1 62.5 %copy-start.7 = (f32[1,15,35]{2,0,1:T(1,128)}, f32[1,15,35]{2,0,1:T(1,128)S(1)}, u32[]{:S(2)}) copy-start(f32[1,15,35]{2,0,1:T(1,128)S(1)} %get-tuple-element.93) | copy-start | bytes 6304
  16.8 4.9 %copy-start.31 = (s32[2,96]{1,0:T(2,128)S(1)}, s32[2,96]{1,0:T(2,128)}, u32[]{:S(2)}) copy-start(s32[2,96]{1,0:T(2,128)} %param.30) | copy-start | bytes 2308
  16.8 19.3 %all-to-all-start = ((f32[4,1,1920]{2,1,0:T(1,128)}), f32[4,1,1920]{2,1,0:T(1,128)S(1)}, u32[]{:S(2)}, u32[]{:S(2)}) async-start(f32[4,1,1920]{2,1,0:T(1,128)} %reshape.663), calls=%async_computation | async-start | bytes 61440 | tf_op jit(solution)/shard_map/all_to_all | solution.py:87
  21.6 0.7 copy-start.29
  21.7 27.6 %copy-start.22 = (pred[96]{0:T(512)(128)(4,1)}, pred[96]{0:T(512)(128)(4,1)S(1)}, u32[]{:S(2)}) copy-start(pred[96]{0:T(512)(128)(4,1)S(1)} %get-tuple-element.59) | copy-start | bytes 292
  21.7 29.1 %copy-start.20 = (pred[96]{0:T(512)(128)(4,1)}, pred[96]{0:T(512)(128)(4,1)S(1)}, u32[]{:S(2)}) copy-start(pred[96]{0:T(512)(128)(4,1)S(1)} %get-tuple-element.98) | copy-start | bytes 292
  22.3 0.6 copy-start.24
  23.1 10.1 %collective-permute-start = (f32[60,96]{0,1:T(8,128)S(1)}, f32[60,96]{0,1:T(8,128)S(1)}, u32[]{:S(2)}, u32[]{:S(2)}) collective-permute-start(f32[60,96]{0,1:T(8,128)S(1)} %select_bitcast_fusion.7), channel_id=1, source_target_pairs={{0,4},{4,8},{8,12},{12,16},{16,20},{20,24},{24,28},{1,5},{5,9},{9,... | collective-permute-start | bytes 69128 | tf_op jit(solution)/shard_map/ppermute | solution.py:19
  27.3 0.6 copy-start.26
  28.7 6.6 %collective-permute-start.1 = (f32[60,96]{0,1:T(8,128)}, f32[60,96]{0,1:T(8,128)}, u32[]{:S(2)}, u32[]{:S(2)}) collective-permute-start(f32[60,96]{0,1:T(8,128)} %select_bitcast_fusion.6), channel_id=1, source_target_pairs={{4,0},{8,4},{12,8},{16,12},{20,16},{24,20},{28,24},{5,1},{9,5},{13... | collective-permute-start | bytes 69128 | tf_op jit(solution)/shard_map/ppermute | solution.py:19
  30.6 9.6 %copy-start.16 = (pred[1024]{0:T(1024)(128)(4,1)}, pred[1024]{0:T(1024)(128)(4,1)S(1)}, u32[]{:S(2)}) copy-start(pred[1024]{0:T(1024)(128)(4,1)S(1)} %compare_and_fusion) | copy-start | bytes 3076
  30.9 0.7 copy-start.19
  30.9 0.9 copy-start.6
  32.5 0.6 copy-start.30
  40.9 0.8 copy-start.5
  49.3 0.7 copy-start.28
  50.9 13.8 %all-to-all-start.1 = ((f32[4,1,1920]{2,1,0:T(1,128)}), f32[4,1,1920]{2,1,0:T(1,128)S(1)}, u32[]{:S(2)}, u32[]{:S(2)}) async-start(f32[4,1,1920]{2,1,0:T(1,128)} %reshape.665), calls=%async_computation.1 | async-start | bytes 61440 | tf_op jit(solution)/shard_map/all_to_all | solution.py:87
  55.4 5.0 %collective-permute-start.2 = (f32[60,96]{0,1:T(8,128)S(1)}, f32[60,96]{0,1:T(8,128)S(1)}, u32[]{:S(2)}, u32[]{:S(2)}) collective-permute-start(f32[60,96]{0,1:T(8,128)S(1)} %select_bitcast_fusion.5), channel_id=1, source_target_pairs={{0,4},{4,8},{8,12},{12,16},{16,20},{20,24},{24,28},{1,5},{5,9},{9,... | collective-permute-start | bytes 69128 | tf_op jit(solution)/shard_map/ppermute | solution.py:19
  58.4 6.3 %collective-permute-start.3 = (f32[60,96]{0,1:T(8,128)S(1)}, f32[60,96]{0,1:T(8,128)S(1)}, u32[]{:S(2)}, u32[]{:S(2)}) collective-permute-start(f32[60,96]{0,1:T(8,128)S(1)} %select_bitcast_fusion.4), channel_id=1, source_target_pairs={{4,0},{8,4},{12,8},{16,12},{20,16},{24,20},{28,24},{5,1},{9,5},{13... | collective-permute-start | bytes 69128 | tf_op jit(solution)/shard_map/ppermute | solution.py:19
  65.5 2.8 %copy-start.17 = (pred[1024]{0:T(1024)(128)(4,1)S(1)}, pred[1024]{0:T(1024)(128)(4,1)}, u32[]{:S(2)}) copy-start(pred[1024]{0:T(1024)(128)(4,1)} %copy-done.16) | copy-start | bytes 3076
  76.7 0.6 copy-start.23
  77.4 0.8 copy-start.21
  78.3 13.3 %all-to-all-start.2 = ((f32[4,1,1920]{2,1,0:T(1,128)}), f32[4,1,1920]{2,1,0:T(1,128)S(1)}, u32[]{:S(2)}, u32[]{:S(2)}) async-start(f32[4,1,1920]{2,1,0:T(1,128)} %reshape.667), calls=%async_computation.2 | async-start | bytes 61440 | tf_op jit(solution)/shard_map/all_to_all | solution.py:87
  82.8 4.4 %collective-permute-start.4 = (f32[60,96]{0,1:T(8,128)S(1)}, f32[60,96]{0,1:T(8,128)S(1)}, u32[]{:S(2)}, u32[]{:S(2)}) collective-permute-start(f32[60,96]{0,1:T(8,128)S(1)} %select_bitcast_fusion.3), channel_id=1, source_target_pairs={{0,4},{4,8},{8,12},{12,16},{16,20},{20,24},{24,28},{1,5},{5,9},{9,... | collective-permute-start | bytes 69128 | tf_op jit(solution)/shard_map/ppermute | solution.py:19
  85.3 6.3 %collective-permute-start.5 = (f32[60,96]{0,1:T(8,128)S(1)}, f32[60,96]{0,1:T(8,128)S(1)}, u32[]{:S(2)}, u32[]{:S(2)}) collective-permute-start(f32[60,96]{0,1:T(8,128)S(1)} %select_bitcast_fusion.2), channel_id=1, source_target_pairs={{4,0},{8,4},{12,8},{16,12},{20,16},{24,20},{28,24},{5,1},{9,5},{13... | collective-permute-start | bytes 69128 | tf_op jit(solution)/shard_map/ppermute | solution.py:19
  95.9 0.7 copy-start.15
  99.5 0.7 copy-start.12
  100.2 0.7 copy-start.10
  100.9 0.7 copy-start.8
  106.7 13.3 %all-to-all-start.3 = ((f32[4,1,1920]{2,1,0:T(1,128)}), f32[4,1,1920]{2,1,0:T(1,128)S(1)}, u32[]{:S(2)}, u32[]{:S(2)}) async-start(f32[4,1,1920]{2,1,0:T(1,128)} %reshape.669), calls=%async_computation.3 | async-start | bytes 61440 | tf_op jit(solution)/shard_map/all_to_all | solution.py:87
  111.2 4.4 %collective-permute-start.6 = (f32[60,96]{0,1:T(8,128)S(1)}, f32[60,96]{0,1:T(8,128)S(1)}, u32[]{:S(2)}, u32[]{:S(2)}) collective-permute-start(f32[60,96]{0,1:T(8,128)S(1)} %select_bitcast_fusion.1), channel_id=1, source_target_pairs={{0,4},{4,8},{8,12},{12,16},{16,20},{20,24},{24,28},{1,5},{5,9},{9,... | collective-permute-start | bytes 69128 | tf_op jit(solution)/shard_map/ppermute | solution.py:19
  113.7 6.3 %collective-permute-start.7 = (f32[60,96]{0,1:T(8,128)S(1)}, f32[60,96]{0,1:T(8,128)S(1)}, u32[]{:S(2)}, u32[]{:S(2)}) collective-permute-start(f32[60,96]{0,1:T(8,128)S(1)} %select_bitcast_fusion), channel_id=1, source_target_pairs={{4,0},{8,4},{12,8},{16,12},{20,16},{24,20},{28,24},{5,1},{9,5},{13... | collective-permute-start | bytes 69128 | tf_op jit(solution)/shard_map/ppermute | solution.py:19
where the time goes:
time: 127 us; the launch traced here: 125 us
  local copies, waits for them, and re-layouts  42.8 us (34%)
  starting transfers between devices  38.3 us (30%)
  matrix products  17.1 us (13%)
  waiting for transfers between devices  15 us (12%)
  other arithmetic  9.86 us (8%)
  between operations  2.35 us (2%)
    ppermute x8, starting transfers between devices, from_behind(): return lax.ppermute(shard, axis, pairs)  19.8 us
    all_to_all x4, starting transfers between devices, gather_faces(): lax.all_to_all(sub_out, 'sub', split_axis=1, concat_axis=1, tiled=True)  18.5 us
    ppermute x8, waiting for transfers between devices, from_behind(): return lax.ppermute(shard, axis, pairs)  15 us
    unnamed x105, local copies, waits for them, and re-layouts  13.5 us
    gather x4, local copies, waits for them, and re-layouts, body(): nbr_traces = jnp.take(trace_pool, neighbours.reshape(-1), axis=1)  11.2 us
    dot_general x25, matrix products, apply_operator(): jnp.dot(joined, mixed_vel.reshape(3 * n_basis, -1), precision=exact_dots)  6.34 us
    dot_general x25, matrix products, apply_operator(): jnp.dot(stacked, pressure, precision=exact_dots).reshape(3, n_basis, -1)  5.98 us
    dot_general x16, matrix products, face_traces(): jnp.einsum('kb,qbe->kqe', face_proj[face_idx], coeffs, precision=exact_dots)  3.34 us
  transfers between devices with their start and end apart: 12, of which 4 were waited for; matrix products, arithmetic and copies ran while one was open for 3% of the time, Pallas kernels for 0%

commit v1 on v0

--- a/solution.py
+++ b/solution.py
@@ -11,6 +11,18 @@
 exact_dots = lax.Precision.HIGHEST
 step_size = 0.8
 sigma_pml = 1.5
+
+
+def exchange_directly(value, axis, split, join):
+    ways, here = (lax.axis_size(axis), lax.axis_index(axis))
+    width = value.shape[split] // ways
+    turned = jnp.roll(value, -here * width, axis=split)
+    got = [lax.slice_in_dim(turned, 0, width, axis=split)]
+    for far in range(1, ways):
+        sent = lax.slice_in_dim(turned, far * width, (far + 1) * width, axis=split)
+        got.append(lax.ppermute(sent, axis, [(d, (d + far) % ways) for d in range(ways)]))
+    line = jnp.concatenate(got[::-1], axis=join)
+    return jnp.roll(line, (here + 1) * got[0].shape[join], axis=join)
 
 
 def from_behind(shard, axis, by):
@@ -84,9 +96,7 @@
         [jnp.take(own_traces, dom_send[0], axis=1), jnp.take(own_traces, dom_send[1], axis=1)]
     )
     sub_out = jnp.take(own_traces, sub_send.reshape(-1), axis=1).reshape(n_chan, n_sub, sub_width)
-    sub_in = lax.all_to_all(sub_out, "sub", split_axis=1, concat_axis=1, tiled=True).reshape(
-        n_chan, n_sub * sub_width
-    )
+    sub_in = exchange_directly(sub_out, "sub", 1, 1).reshape(n_chan, n_sub * sub_width)
     from_below = from_behind(dom_out[1], "dom", 1)
     from_above = from_behind(dom_out[0], "dom", -1)
     return jnp.concatenate([own_traces, from_below, from_above, sub_in], axis=1)

time: 127 us -> 118 us (0.929)
  local copies, waits for them, and re-layouts: 42.8 us -> 39.2 us
  starting transfers between devices: 38.3 us -> 36.2 us
  other arithmetic: 9.86 us -> 7.93 us
  waiting for transfers between devices: 15 us -> 13.5 us
    all_to_all x4 -> x0, starting transfers between devices: 18.5 us -> none  [gather_faces(): lax.all_to_all(sub_out, 'sub', split_axis=1, concat_axis=1, tiled=True)]
    ppermute x0 -> x12, starting transfers between devices: none -> 14.9 us  [exchange_directly(): lax.ppermute(sent, axis, [(d, (d + far) % ways) for d in range(ways)])]
    unnamed x105 -> x99, local copies, waits for them, and re-layouts: 13.5 us -> 10.6 us
    all_to_all x4 -> x0, other arithmetic: 2.57 us -> none  [gather_faces(): lax.all_to_all(sub_out, 'sub', split_axis=1, concat_axis=1, tiled=True)]
    ppermute x8, waiting for transfers between devices: 15 us -> 13.5 us  [from_behind(): return lax.ppermute(shard, axis, pairs)]
    ppermute x8, starting transfers between devices: 19.8 us -> 21.2 us  [from_behind(): return lax.ppermute(shard, axis, pairs)]
  transfers between devices with their start and end apart: 12 -> 20, of which waited for: 4 -> 4; matrix products, arithmetic and copies ran while one was open for 3% -> 3% of each run, Pallas kernels for 0% -> 0%
where the time goes in v1:
time: 118 us; the launch traced here: 116 us
  local copies, waits for them, and re-layouts  39.2 us (33%)
  starting transfers between devices  36.2 us (31%)
  matrix products  17.1 us (14%)
  waiting for transfers between devices  13.5 us (11%)
  other arithmetic  7.93 us (7%)
  between operations  2.56 us (2%)
    ppermute x8, starting transfers between devices, from_behind(): return lax.ppermute(shard, axis, pairs)  21.2 us
    ppermute x12, starting transfers between devices, exchange_directly(): lax.ppermute(sent, axis, [(d, (d + far) % ways) for d in range(ways)])  14.9 us
    ppermute x8, waiting for transfers between devices, from_behind(): return lax.ppermute(shard, axis, pairs)  13.5 us
    gather x4, local copies, waits for them, and re-layouts, body(): nbr_traces = jnp.take(trace_pool, neighbours.reshape(-1), axis=1)  11.2 us
    unnamed x99, local copies, waits for them, and re-layouts  10.6 us
    dot_general x25, matrix products, apply_operator(): jnp.dot(joined, mixed_vel.reshape(3 * n_basis, -1), precision=exact_dots)  6.34 us
    dot_general x25, matrix products, apply_operator(): jnp.dot(stacked, pressure, precision=exact_dots).reshape(3, n_basis, -1)  5.97 us
    dot_general x16, matrix products, face_traces(): jnp.einsum('kb,qbe->kqe', face_proj[face_idx], coeffs, precision=exact_dots)  3.34 us
  transfers between devices with their start and end apart: 20, of which 4 were waited for; matrix products, arithmetic and copies ran while one was open for 3% of the time, Pallas kernels for 0%

profile of v1, /device:TPU:11, one launch (start us, length us, event | category | flops | bytes accessed | tf_op | source)
XLA Modules:
  0.0 116.4 jit_solution(2892027966012171664)
XLA Ops:
  0.0 0.7 copy-done.31
  0.8 0.9 reshape.662
  1.7 0.9 slice.174
  2.9 0.6 copy-done.34
  3.7 0.6 copy-done.4
  4.3 0.6 divide_sqrt_fusion
  5.0 0.6 copy-done.2
  7.1 0.8 slice-done
  9.3 0.7 copy-done.13
  10.8 0.8 multiply_reduce_fusion.1
  15.3 0.6 gather_fusion.2
  16.1 0.6 fusion.215
  16.7 1.3 %collective-permute-start.4 = (f32[60,1,32]{0,2,1:T(8,128)}, f32[60,1,32]{0,2,1:T(8,128)}, u32[]{:S(2)}, u32[]{:S(2)}) collective-permute-start(f32[60,1,32]{0,2,1:T(8,128)} %get-tuple-element.105), channel_id=1, source_target_pairs={{0,1},{1,2},{2,3},{3,0},{4,5},{5,6},{6,7},{7,4},{8,9},{9,10},{10,1... | collective-permute-start | bytes 23048 | tf_op jit(solution)/shard_map/ppermute | solution.py:23
  18.0 1.0 collective-permute-start.3
  19.0 1.5 %collective-permute-start.2 = (f32[60,1,32]{0,2,1:T(8,128)}, f32[60,1,32]{0,2,1:T(8,128)}, u32[]{:S(2)}, u32[]{:S(2)}) collective-permute-start(f32[60,1,32]{0,2,1:T(8,128)} %get-tuple-element.107), channel_id=1, source_target_pairs={{0,3},{1,0},{2,1},{3,2},{4,7},{5,4},{6,5},{7,6},{8,11},{9,8},{10,9... | collective-permute-start | bytes 23048 | tf_op jit(solution)/shard_map/ppermute | solution.py:23
  20.5 0.6 gather_fusion
  21.3 4.5 %collective-permute-start = (f32[60,96]{0,1:T(8,128)S(1)}, f32[60,96]{0,1:T(8,128)S(1)}, u32[]{:S(2)}, u32[]{:S(2)}) collective-permute-start(f32[60,96]{0,1:T(8,128)S(1)} %select_bitcast_fusion.7), channel_id=1, source_target_pairs={{0,4},{4,8},{8,12},{12,16},{16,20},{20,24},{24,28},{1,5},{5,9},{9,... | collective-permute-start | bytes 69128 | tf_op jit(solution)/shard_map/ppermute | solution.py:31
  25.8 0.6 gather_fusion.1
  26.5 1.9 %collective-permute-start.1 = (f32[60,96]{0,1:T(8,128)S(1)}, f32[60,96]{0,1:T(8,128)}, u32[]{:S(2)}, u32[]{:S(2)}) collective-permute-start(f32[60,96]{0,1:T(8,128)S(1)} %select_bitcast_fusion.6), channel_id=1, source_target_pairs={{4,0},{8,4},{12,8},{16,12},{20,16},{24,20},{28,24},{5,1},{9,5},{13... | collective-permute-start | bytes 69128 | tf_op jit(solution)/shard_map/ppermute | solution.py:31
  28.8 0.7 copy-done.19
  30.3 0.6 copy-done.30
  31.1 0.9 fusion.152
  32.0 0.9 collective-permute-done.1
  32.9 0.8 constant_dynamic-update-slice_fusion.1
  33.8 2.8 %gather_fusion.3 = f32[1024,60]{1,0:T(8,128)S(1)} fusion(f32[60,1344]{0,1:T(8,128)S(1)} %constant_dynamic-update-slice_fusion, s32[1024]{0:T(1024)S(1)} %get-tuple-element.119), kind=kCustom, calls=%fused_computation.2.clone | custom fusion | bytes 495616 | tf_op jit(solution)/shard_map/jit(_take)/gather | solution.py:136
  37.3 0.7 copy-done.5
  38.0 0.3 fusion.98
  43.0 0.7 gather_fusion.5
  43.7 0.6 gather_fusion.4
  44.4 0.8 gather_fusion.6
  45.6 0.5 copy-done.28
  46.6 3.1 %collective-permute-start.8 = (f32[60,1,32]{0,2,1:T(8,128)S(1)}, f32[60,1,32]{0,2,1:T(8,128)S(1)}, u32[]{:S(2)}, u32[]{:S(2)}) collective-permute-start(f32[60,1,32]{0,2,1:T(8,128)S(1)} %get-tuple-element.102), channel_id=1, source_target_pairs={{0,2},{1,3},{2,0},{3,1},{4,6},{5,7},{6,4},{7,5},{8,10},{9,11},{10,... | collective-permute-start | bytes 23048 | tf_op jit(solution)/shard_map/ppermute | solution.py:23
  49.8 4.2 %collective-permute-start.5 = (f32[60,96]{0,1:T(8,128)S(1)}, f32[60,96]{0,1:T(8,128)S(1)}, u32[]{:S(2)}, u32[]{:S(2)}) collective-permute-start(f32[60,96]{0,1:T(8,128)S(1)} %select_bitcast_fusion.5), channel_id=1, source_target_pairs={{0,4},{4,8},{8,12},{12,16},{16,20},{20,24},{24,28},{1,5},{5,9},{9,... | collective-permute-start | bytes 69128 | tf_op jit(solution)/shard_map/ppermute | solution.py:31
  53.9 1.9 %collective-permute-start.6 = (f32[60,96]{0,1:T(8,128)S(1)}, f32[60,96]{0,1:T(8,128)S(1)}, u32[]{:S(2)}, u32[]{:S(2)}) collective-permute-start(f32[60,96]{0,1:T(8,128)S(1)} %select_bitcast_fusion.4), channel_id=1, source_target_pairs={{4,0},{8,4},{12,8},{16,12},{20,16},{24,20},{28,24},{5,1},{9,5},{13... | collective-permute-start | bytes 69128 | tf_op jit(solution)/shard_map/ppermute | solution.py:31
  56.1 4.2 %collective-permute-done.6 = f32[60,96]{0,1:T(8,128)S(1)} collective-permute-done((f32[60,96]{0,1:T(8,128)S(1)}, f32[60,96]{0,1:T(8,128)S(1)}, u32[]{:S(2)}, u32[]{:S(2)}) %collective-permute-start.6) | collective-permute-done | bytes 23072 | tf_op jit(solution)/shard_map/ppermute | solution.py:31
  60.2 2.8 %gather_fusion.7 = f32[1024,60]{1,0:T(8,128)S(1)} fusion(f32[60,1344]{0,1:T(8,128)S(1)} %constant_dynamic-update-slice_fusion.7, s32[1024]{0:T(1024)S(1)} %get-tuple-element.119), kind=kCustom, calls=%fused_computation.13.clone | custom fusion | bytes 495616 | tf_op jit(solution)/shard_map/jit(_take)/gather | solution.py:136
  63.8 0.3 fusion.104
  68.8 0.7 gather_fusion.9
  69.5 0.7 gather_fusion.8
  70.3 0.8 gather_fusion.10
  71.4 0.6 copy-done.23
  72.4 1.8 %collective-permute-start.14 = (f32[60,1,32]{0,2,1:T(8,128)S(1)}, f32[60,1,32]{0,2,1:T(8,128)S(1)}, u32[]{:S(2)}, u32[]{:S(2)}) collective-permute-start(f32[60,1,32]{0,2,1:T(8,128)S(1)} %get-tuple-element.97), channel_id=1, source_target_pairs={{0,1},{1,2},{2,3},{3,0},{4,5},{5,6},{6,7},{7,4},{8,9},{9,10},{10,1... | collective-permute-start | bytes 23048 | tf_op jit(solution)/shard_map/ppermute | solution.py:23
  74.2 1.5 %collective-permute-start.13 = (f32[60,1,32]{0,2,1:T(8,128)S(1)}, f32[60,1,32]{0,2,1:T(8,128)S(1)}, u32[]{:S(2)}, u32[]{:S(2)}) collective-permute-start(f32[60,1,32]{0,2,1:T(8,128)S(1)} %get-tuple-element.98), channel_id=1, source_target_pairs={{0,2},{1,3},{2,0},{3,1},{4,6},{5,7},{6,4},{7,5},{8,10},{9,11},{10,... | collective-permute-start | bytes 23048 | tf_op jit(solution)/shard_map/ppermute | solution.py:23
  75.7 2.4 %collective-permute-start.10 = (f32[60,96]{0,1:T(8,128)S(1)}, f32[60,96]{0,1:T(8,128)S(1)}, u32[]{:S(2)}, u32[]{:S(2)}) collective-permute-start(f32[60,96]{0,1:T(8,128)S(1)} %select_bitcast_fusion.3), channel_id=1, source_target_pairs={{0,4},{4,8},{8,12},{12,16},{16,20},{20,24},{24,28},{1,5},{5,9},{9,... | collective-permute-start | bytes 69128 | tf_op jit(solution)/shard_map/ppermute | solution.py:31
  78.2 1.9 %collective-permute-start.11 = (f32[60,96]{0,1:T(8,128)S(1)}, f32[60,96]{0,1:T(8,128)S(1)}, u32[]{:S(2)}, u32[]{:S(2)}) collective-permute-start(f32[60,96]{0,1:T(8,128)S(1)} %select_bitcast_fusion.2), channel_id=1, source_target_pairs={{4,0},{8,4},{12,8},{16,12},{20,16},{24,20},{28,24},{5,1},{9,5},{13... | collective-permute-start | bytes 69128 | tf_op jit(solution)/shard_map/ppermute | solution.py:31
  80.3 4.2 %collective-permute-done.11 = f32[60,96]{0,1:T(8,128)S(1)} collective-permute-done((f32[60,96]{0,1:T(8,128)S(1)}, f32[60,96]{0,1:T(8,128)S(1)}, u32[]{:S(2)}, u32[]{:S(2)}) %collective-permute-start.11) | collective-permute-done | bytes 23072 | tf_op jit(solution)/shard_map/ppermute | solution.py:31
  84.5 2.8 %gather_fusion.11 = f32[1024,60]{1,0:T(8,128)S(1)} fusion(f32[60,1344]{0,1:T(8,128)S(1)} %constant_dynamic-update-slice_fusion.14, s32[1024]{0:T(1024)S(1)} %get-tuple-element.119), kind=kCustom, calls=%fused_computation.14.clone | custom fusion | bytes 495616 | tf_op jit(solution)/shard_map/jit(_take)/gather | solution.py:136
  88.0 0.7 copy-done.15
  88.7 0.3 fusion.110
  91.8 0.5 copy-done.12
  92.5 0.5 copy-done.10
  93.2 0.5 copy-done.8
  95.2 0.7 gather_fusion.13
  95.9 0.7 gather_fusion.12
  96.7 0.8 gather_fusion.14
  98.0 0.5 copy-done.21
  98.6 1.8 %collective-permute-start.19 = (f32[60,1,32]{0,2,1:T(8,128)S(1)}, f32[60,1,32]{0,2,1:T(8,128)S(1)}, u32[]{:S(2)}, u32[]{:S(2)}) collective-permute-start(f32[60,1,32]{0,2,1:T(8,128)S(1)} %get-tuple-element.93), channel_id=1, source_target_pairs={{0,1},{1,2},{2,3},{3,0},{4,5},{5,6},{6,7},{7,4},{8,9},{9,10},{10,1... | collective-permute-start | bytes 23048 | tf_op jit(solution)/shard_map/ppermute | solution.py:23
  100.4 2.6 %collective-permute-start.18 = (f32[60,1,32]{0,2,1:T(8,128)S(1)}, f32[60,1,32]{0,2,1:T(8,128)S(1)}, u32[]{:S(2)}, u32[]{:S(2)}) collective-permute-start(f32[60,1,32]{0,2,1:T(8,128)S(1)} %get-tuple-element.94), channel_id=1, source_target_pairs={{0,2},{1,3},{2,0},{3,1},{4,6},{5,7},{6,4},{7,5},{8,10},{9,11},{10,... | collective-permute-start | bytes 23048 | tf_op jit(solution)/shard_map/ppermute | solution.py:23
  103.1 2.4 %collective-permute-start.15 = (f32[60,96]{0,1:T(8,128)S(1)}, f32[60,96]{0,1:T(8,128)S(1)}, u32[]{:S(2)}, u32[]{:S(2)}) collective-permute-start(f32[60,96]{0,1:T(8,128)S(1)} %select_bitcast_fusion.1), channel_id=1, source_target_pairs={{0,4},{4,8},{8,12},{12,16},{16,20},{20,24},{24,28},{1,5},{5,9},{9,... | collective-permute-start | bytes 69128 | tf_op jit(solution)/shard_map/ppermute | solution.py:31
  105.5 1.9 %collective-permute-start.16 = (f32[60,96]{0,1:T(8,128)S(1)}, f32[60,96]{0,1:T(8,128)S(1)}, u32[]{:S(2)}, u32[]{:S(2)}) collective-permute-start(f32[60,96]{0,1:T(8,128)S(1)} %select_bitcast_fusion), channel_id=1, source_target_pairs={{4,0},{8,4},{12,8},{16,12},{20,16},{24,20},{28,24},{5,1},{9,5},{13... | collective-permute-start | bytes 69128 | tf_op jit(solution)/shard_map/ppermute | solution.py:31
  107.7 4.2 %collective-permute-done.16 = f32[60,96]{0,1:T(8,128)S(1)} collective-permute-done((f32[60,96]{0,1:T(8,128)S(1)}, f32[60,96]{0,1:T(8,128)S(1)}, u32[]{:S(2)}, u32[]{:S(2)}) %collective-permute-start.16) | collective-permute-done | bytes 23072 | tf_op jit(solution)/shard_map/ppermute | solution.py:31
  111.9 2.8 %gather_fusion.15 = f32[1024,60]{1,0:T(8,128)S(1)} fusion(f32[60,1344]{0,1:T(8,128)S(1)} %constant_dynamic-update-slice_fusion.21, s32[1024]{0:T(1024)S(1)} %get-tuple-element.119), kind=kCustom, calls=%fused_computation.15.clone | custom fusion | bytes 495616 | tf_op jit(solution)/shard_map/jit(_take)/gather | solution.py:136
  115.4 0.4 subtract_select_fusion
  115.8 0.7 reshape.447
  (385 shorter events, 27.4 us)
Async XLA Ops:
  0.0 0.7 copy-start.31
  0.8 15.1 %copy-start.27 = (pred[128]{0:T(512)(128)(4,1)}, pred[128]{0:T(512)(128)(4,1)S(1)}, u32[]{:S(2)}) copy-start(pred[128]{0:T(512)(128)(4,1)S(1)} %compare_and_fusion.1) | copy-start | bytes 388
  0.8 1.8 %copy-start.1 = (f32[140,256]{1,0:T(8,128)S(1)}, f32[140,256]{1,0:T(8,128)}, u32[]{:S(2)}) copy-start(f32[140,256]{1,0:T(8,128)} %param.21) | copy-start | bytes 430084
  1.7 0.9 copy-start
  2.9 0.7 copy-start.34
  2.9 0.7 copy-start.18
  3.6 0.7 copy-start.4
  3.6 0.7 copy-start.14
  3.7 0.7 copy-start.33
  5.0 0.7 copy-start.2
  7.0 0.9 slice-start
  9.3 0.8 copy-start.13
  9.3 0.9 copy-start.3
  10.0 5.2 %copy-start.25 = (s32[1024]{0:T(1024)}, s32[1024]{0:T(1024)S(1)}, u32[]{:S(2)}) copy-start(s32[1024]{0:T(1024)S(1)} %pad_clamp_fusion) | copy-start | bytes 12292
  10.1 56.8 %copy-start.11 = (f32[1,15,35]{2,0,1:T(1,128)}, f32[1,15,35]{2,0,1:T(1,128)S(1)}, u32[]{:S(2)}) copy-start(f32[1,15,35]{2,0,1:T(1,128)S(1)} %get-tuple-element.108) | copy-start | bytes 6304
  10.1 57.0 %copy-start.9 = (f32[1,15,35]{2,0,1:T(1,128)}, f32[1,15,35]{2,0,1:T(1,128)S(1)}, u32[]{:S(2)}) copy-start(f32[1,15,35]{2,0,1:T(1,128)S(1)} %get-tuple-element.109) | copy-start | bytes 6304
  10.1 57.2 %copy-start.7 = (f32[1,15,35]{2,0,1:T(1,128)}, f32[1,15,35]{2,0,1:T(1,128)S(1)}, u32[]{:S(2)}) copy-start(f32[1,15,35]{2,0,1:T(1,128)S(1)} %get-tuple-element.110) | copy-start | bytes 6304
  15.9 4.5 %copy-start.32 = (s32[2,96]{1,0:T(2,128)S(1)}, s32[2,96]{1,0:T(2,128)}, u32[]{:S(2)}) copy-start(s32[2,96]{1,0:T(2,128)} %param.32) | copy-start | bytes 2308
  16.7 3.8 %copy-start.29 = (s32[4,256]{1,0:T(4,128)S(1)}, s32[4,256]{1,0:T(4,128)}, u32[]{:S(2)}) copy-start(s32[4,256]{1,0:T(4,128)} %param.31) | copy-start | bytes 12292
  16.7 14.4 %collective-permute-start.4 = (f32[60,1,32]{0,2,1:T(8,128)}, f32[60,1,32]{0,2,1:T(8,128)}, u32[]{:S(2)}, u32[]{:S(2)}) collective-permute-start(f32[60,1,32]{0,2,1:T(8,128)} %get-tuple-element.105), channel_id=1, source_target_pairs={{0,1},{1,2},{2,3},{3,0},{4,5},{5,6},{6,7},{7,4},{8,9},{9,10},{10,1... | collective-permute-start | bytes 23048 | tf_op jit(solution)/shard_map/ppermute | solution.py:23
  18.0 13.1 %collective-permute-start.3 = (f32[60,1,32]{0,2,1:T(8,128)}, f32[60,1,32]{0,2,1:T(8,128)}, u32[]{:S(2)}, u32[]{:S(2)}) collective-permute-start(f32[60,1,32]{0,2,1:T(8,128)} %get-tuple-element.106), channel_id=1, source_target_pairs={{0,2},{1,3},{2,0},{3,1},{4,6},{5,7},{6,4},{7,5},{8,10},{9,11},{10,... | collective-permute-start | bytes 23048 | tf_op jit(solution)/shard_map/ppermute | solution.py:23
  19.0 12.1 %collective-permute-start.2 = (f32[60,1,32]{0,2,1:T(8,128)}, f32[60,1,32]{0,2,1:T(8,128)}, u32[]{:S(2)}, u32[]{:S(2)}) collective-permute-start(f32[60,1,32]{0,2,1:T(8,128)} %get-tuple-element.107), channel_id=1, source_target_pairs={{0,3},{1,0},{2,1},{3,2},{4,7},{5,4},{6,5},{7,6},{8,11},{9,8},{10,9... | collective-permute-start | bytes 23048 | tf_op jit(solution)/shard_map/ppermute | solution.py:23
  20.5 25.0 %copy-start.22 = (pred[96]{0:T(512)(128)(4,1)}, pred[96]{0:T(512)(128)(4,1)S(1)}, u32[]{:S(2)}) copy-start(pred[96]{0:T(512)(128)(4,1)S(1)} %get-tuple-element.60) | copy-start | bytes 292
  20.5 51.8 %copy-start.20 = (pred[96]{0:T(512)(128)(4,1)}, pred[96]{0:T(512)(128)(4,1)S(1)}, u32[]{:S(2)}) copy-start(pred[96]{0:T(512)(128)(4,1)S(1)} %get-tuple-element.115) | copy-start | bytes 292
  20.5 23.2 %copy-start.24 = (s32[1024]{0:T(1024)}, s32[1024]{0:T(1024)S(1)}, u32[]{:S(2)}) copy-start(s32[1024]{0:T(1024)S(1)} %get-tuple-element.118) | copy-start | bytes 12292
  21.3 10.7 %collective-permute-start = (f32[60,96]{0,1:T(8,128)S(1)}, f32[60,96]{0,1:T(8,128)S(1)}, u32[]{:S(2)}, u32[]{:S(2)}) collective-permute-start(f32[60,96]{0,1:T(8,128)S(1)} %select_bitcast_fusion.7), channel_id=1, source_target_pairs={{0,4},{4,8},{8,12},{12,16},{16,20},{20,24},{24,28},{1,5},{5,9},{9,... | collective-permute-start | bytes 69128 | tf_op jit(solution)/shard_map/ppermute | solution.py:31
  25.8 0.6 copy-start.26
  26.5 6.4 %collective-permute-start.1 = (f32[60,96]{0,1:T(8,128)S(1)}, f32[60,96]{0,1:T(8,128)}, u32[]{:S(2)}, u32[]{:S(2)}) collective-permute-start(f32[60,96]{0,1:T(8,128)S(1)} %select_bitcast_fusion.6), channel_id=1, source_target_pairs={{4,0},{8,4},{12,8},{16,12},{20,16},{24,20},{28,24},{5,1},{9,5},{13... | collective-permute-start | bytes 69128 | tf_op jit(solution)/shard_map/ppermute | solution.py:31
  28.5 58.8 %copy-start.16 = (pred[1024]{0:T(1024)(128)(4,1)}, pred[1024]{0:T(1024)(128)(4,1)S(1)}, u32[]{:S(2)}) copy-start(pred[1024]{0:T(1024)(128)(4,1)S(1)} %compare_and_fusion) | copy-start | bytes 3076
  28.7 0.7 copy-start.19
  28.8 0.9 copy-start.6
  30.3 0.6 copy-start.30
  37.3 0.8 copy-start.5
  45.5 0.6 copy-start.28
  46.4 9.5 %collective-permute-start.9 = (f32[60,1,32]{0,2,1:T(8,128)S(1)}, f32[60,1,32]{0,2,1:T(8,128)S(1)}, u32[]{:S(2)}, u32[]{:S(2)}) collective-permute-start(f32[60,1,32]{0,2,1:T(8,128)S(1)} %get-tuple-element.101), channel_id=1, source_target_pairs={{0,1},{1,2},{2,3},{3,0},{4,5},{5,6},{6,7},{7,4},{8,9},{9,10},{10,1... | collective-permute-start | bytes 23048 | tf_op jit(solution)/shard_map/ppermute | solution.py:23
  46.6 9.3 %collective-permute-start.8 = (f32[60,1,32]{0,2,1:T(8,128)S(1)}, f32[60,1,32]{0,2,1:T(8,128)S(1)}, u32[]{:S(2)}, u32[]{:S(2)}) collective-permute-start(f32[60,1,32]{0,2,1:T(8,128)S(1)} %get-tuple-element.102), channel_id=1, source_target_pairs={{0,2},{1,3},{2,0},{3,1},{4,6},{5,7},{6,4},{7,5},{8,10},{9,11},{10,... | collective-permute-start | bytes 23048 | tf_op jit(solution)/shard_map/ppermute | solution.py:23
  49.8 6.2 %collective-permute-start.7 = (f32[60,1,32]{0,2,1:T(8,128)S(1)}, f32[60,1,32]{0,2,1:T(8,128)S(1)}, u32[]{:S(2)}, u32[]{:S(2)}) collective-permute-start(f32[60,1,32]{0,2,1:T(8,128)S(1)} %get-tuple-element.103), channel_id=1, source_target_pairs={{0,3},{1,0},{2,1},{3,2},{4,7},{5,4},{6,5},{7,6},{8,11},{9,8},{10,9... | collective-permute-start | bytes 23048 | tf_op jit(solution)/shard_map/ppermute | solution.py:23
  49.8 6.3 %collective-permute-start.5 = (f32[60,96]{0,1:T(8,128)S(1)}, f32[60,96]{0,1:T(8,128)S(1)}, u32[]{:S(2)}, u32[]{:S(2)}) collective-permute-start(f32[60,96]{0,1:T(8,128)S(1)} %select_bitcast_fusion.5), channel_id=1, source_target_pairs={{0,4},{4,8},{8,12},{12,16},{16,20},{20,24},{24,28},{1,5},{5,9},{9,... | collective-permute-start | bytes 69128 | tf_op jit(solution)/shard_map/ppermute | solution.py:31
  53.9 6.3 %collective-permute-start.6 = (f32[60,96]{0,1:T(8,128)S(1)}, f32[60,96]{0,1:T(8,128)S(1)}, u32[]{:S(2)}, u32[]{:S(2)}) collective-permute-start(f32[60,96]{0,1:T(8,128)S(1)} %select_bitcast_fusion.4), channel_id=1, source_target_pairs={{4,0},{8,4},{12,8},{16,12},{20,16},{24,20},{28,24},{5,1},{9,5},{13... | collective-permute-start | bytes 69128 | tf_op jit(solution)/shard_map/ppermute | solution.py:31
  71.4 0.7 copy-start.23
  72.4 7.8 %collective-permute-start.14 = (f32[60,1,32]{0,2,1:T(8,128)S(1)}, f32[60,1,32]{0,2,1:T(8,128)S(1)}, u32[]{:S(2)}, u32[]{:S(2)}) collective-permute-start(f32[60,1,32]{0,2,1:T(8,128)S(1)} %get-tuple-element.97), channel_id=1, source_target_pairs={{0,1},{1,2},{2,3},{3,0},{4,5},{5,6},{6,7},{7,4},{8,9},{9,10},{10,1... | collective-permute-start | bytes 23048 | tf_op jit(solution)/shard_map/ppermute | solution.py:23
  74.2 6.0 %collective-permute-start.13 = (f32[60,1,32]{0,2,1:T(8,128)S(1)}, f32[60,1,32]{0,2,1:T(8,128)S(1)}, u32[]{:S(2)}, u32[]{:S(2)}) collective-permute-start(f32[60,1,32]{0,2,1:T(8,128)S(1)} %get-tuple-element.98), channel_id=1, source_target_pairs={{0,2},{1,3},{2,0},{3,1},{4,6},{5,7},{6,4},{7,5},{8,10},{9,11},{10,... | collective-permute-start | bytes 23048 | tf_op jit(solution)/shard_map/ppermute | solution.py:23
  75.7 4.5 %collective-permute-start.12 = (f32[60,1,32]{0,2,1:T(8,128)S(1)}, f32[60,1,32]{0,2,1:T(8,128)S(1)}, u32[]{:S(2)}, u32[]{:S(2)}) collective-permute-start(f32[60,1,32]{0,2,1:T(8,128)S(1)} %get-tuple-element.99), channel_id=1, source_target_pairs={{0,3},{1,0},{2,1},{3,2},{4,7},{5,4},{6,5},{7,6},{8,11},{9,8},{10,9... | collective-permute-start | bytes 23048 | tf_op jit(solution)/shard_map/ppermute | solution.py:23
  75.7 4.6 %collective-permute-start.10 = (f32[60,96]{0,1:T(8,128)S(1)}, f32[60,96]{0,1:T(8,128)S(1)}, u32[]{:S(2)}, u32[]{:S(2)}) collective-permute-start(f32[60,96]{0,1:T(8,128)S(1)} %select_bitcast_fusion.3), channel_id=1, source_target_pairs={{0,4},{4,8},{8,12},{12,16},{16,20},{20,24},{24,28},{1,5},{5,9},{9,... | collective-permute-start | bytes 69128 | tf_op jit(solution)/shard_map/ppermute | solution.py:31
  78.2 6.3 %collective-permute-start.11 = (f32[60,96]{0,1:T(8,128)S(1)}, f32[60,96]{0,1:T(8,128)S(1)}, u32[]{:S(2)}, u32[]{:S(2)}) collective-permute-start(f32[60,96]{0,1:T(8,128)S(1)} %select_bitcast_fusion.2), channel_id=1, source_target_pairs={{4,0},{8,4},{12,8},{16,12},{20,16},{24,20},{28,24},{5,1},{9,5},{13... | collective-permute-start | bytes 69128 | tf_op jit(solution)/shard_map/ppermute | solution.py:31
  88.0 0.7 copy-start.15
  91.6 0.7 copy-start.12
  92.3 0.7 copy-start.10
  93.0 0.7 copy-start.8
  97.9 0.6 copy-start.21
  98.6 8.9 %collective-permute-start.19 = (f32[60,1,32]{0,2,1:T(8,128)S(1)}, f32[60,1,32]{0,2,1:T(8,128)S(1)}, u32[]{:S(2)}, u32[]{:S(2)}) collective-permute-start(f32[60,1,32]{0,2,1:T(8,128)S(1)} %get-tuple-element.93), channel_id=1, source_target_pairs={{0,1},{1,2},{2,3},{3,0},{4,5},{5,6},{6,7},{7,4},{8,9},{9,10},{10,1... | collective-permute-start | bytes 23048 | tf_op jit(solution)/shard_map/ppermute | solution.py:23
  100.4 7.1 %collective-permute-start.18 = (f32[60,1,32]{0,2,1:T(8,128)S(1)}, f32[60,1,32]{0,2,1:T(8,128)S(1)}, u32[]{:S(2)}, u32[]{:S(2)}) collective-permute-start(f32[60,1,32]{0,2,1:T(8,128)S(1)} %get-tuple-element.94), channel_id=1, source_target_pairs={{0,2},{1,3},{2,0},{3,1},{4,6},{5,7},{6,4},{7,5},{8,10},{9,11},{10,... | collective-permute-start | bytes 23048 | tf_op jit(solution)/shard_map/ppermute | solution.py:23
  103.1 4.5 %collective-permute-start.17 = (f32[60,1,32]{0,2,1:T(8,128)S(1)}, f32[60,1,32]{0,2,1:T(8,128)S(1)}, u32[]{:S(2)}, u32[]{:S(2)}) collective-permute-start(f32[60,1,32]{0,2,1:T(8,128)S(1)} %get-tuple-element.95), channel_id=1, source_target_pairs={{0,3},{1,0},{2,1},{3,2},{4,7},{5,4},{6,5},{7,6},{8,11},{9,8},{10,9... | collective-permute-start | bytes 23048 | tf_op jit(solution)/shard_map/ppermute | solution.py:23
  103.1 4.6 %collective-permute-start.15 = (f32[60,96]{0,1:T(8,128)S(1)}, f32[60,96]{0,1:T(8,128)S(1)}, u32[]{:S(2)}, u32[]{:S(2)}) collective-permute-start(f32[60,96]{0,1:T(8,128)S(1)} %select_bitcast_fusion.1), channel_id=1, source_target_pairs={{0,4},{4,8},{8,12},{12,16},{16,20},{20,24},{24,28},{1,5},{5,9},{9,... | collective-permute-start | bytes 69128 | tf_op jit(solution)/shard_map/ppermute | solution.py:31
  105.5 6.3 %collective-permute-start.16 = (f32[60,96]{0,1:T(8,128)S(1)}, f32[60,96]{0,1:T(8,128)S(1)}, u32[]{:S(2)}, u32[]{:S(2)}) collective-permute-start(f32[60,96]{0,1:T(8,128)S(1)} %select_bitcast_fusion), channel_id=1, source_target_pairs={{4,0},{8,4},{12,8},{16,12},{20,16},{24,20},{28,24},{5,1},{9,5},{13... | collective-permute-start | bytes 69128 | tf_op jit(solution)/shard_map/ppermute | solution.py:31
  111.8 2.8 %copy-start.17 = (pred[1024]{0:T(1024)(128)(4,1)S(1)}, pred[1024]{0:T(1024)(128)(4,1)}, u32[]{:S(2)}) copy-start(pred[1024]{0:T(1024)(128)(4,1)} %copy-done.16) | copy-start | bytes 3076
